TPU v7x, 512 devices: a whole 4x4x16 slice. The times are simulated.
512 devices in a mesh: walk: 64 (over z, y), col: 8 (over x, core).
Axes of the slice: x: 4, y: 4, z: 16, core: 2. Of those that a mesh axis runs over, the one named last changes fastest.
Arguments:
- jacobian: float32 [384, 524288], P('walk', 'col'), may hold values from -25 to 25
- prev_update: float32 [8, 65536], P('col', 'walk'), may hold values from -6 to 6
- base_energy: float32 [384], P('walk'), may hold values from -6 to 6
- elec_pos: float32 [384, 3, 66], P('walk'), may hold values from -8 to 8
- atom_pos: float32 [3, 21], replicated, may hold values from -6 to 6
- quad_ratio: float32 [384, 21, 66, 12], P('walk'), may hold values from -1.2 to 1.2
- rotation: int32 [384, 66], P('walk'), may hold values from 0 to 15
- channels: int32 [21], replicated, may hold values from 1 to 3
- ecp_coef: float32 [21, 3], replicated, may hold values from 0.5 to 2
- ecp_expo: float32 [21, 3], replicated, may hold values from 0.2 to 2
Outputs:
- local_energy: float32 [384], P('walk')
- update: float32 [8, 65536], P('col', 'walk')
All inputs are finite; a program needn't handle non-finite values.
Results may differ from a plain program's by a relative error of at most 0.0003.
Values sent between devices are 32-bit elements; how exact they have to be, the bound alone decides.
No kernel may reach another device: no remote copies, remote signals or barrier semaphores. Data moves between devices by JAX's collectives and lax.ppermute only.
A program may use at most 64 MiB of HBM per device.

v0:
```python
import math
import jax
import jax.numpy as jnp
from jax import lax
from jax.sharding import PartitionSpec as P

NROT = 16
momentum = 0.9
damping = 0.1


def icosa_points():
    golden = (1.0 + math.sqrt(5.0)) / 2.0
    length = math.sqrt(1.0 + golden * golden)
    rows = []
    for first in (-1.0, 1.0):
        for second in (-golden, golden):
            rows.append((0.0, first / length, second / length))
            rows.append((first / length, second / length, 0.0))
            rows.append((second / length, 0.0, first / length))
    return jnp.asarray(rows, dtype=jnp.float32).T


def rotation_table(count):
    angle = jnp.arange(count, dtype=jnp.float32)
    turn_z = 2.0 * math.pi * angle / count
    turn_x = 0.9 * angle
    cz, sz = (jnp.cos(turn_z), jnp.sin(turn_z))
    cx, sx = (jnp.cos(turn_x), jnp.sin(turn_x))
    zeros = jnp.zeros_like(cz)
    matrix = jnp.stack(
        [
            jnp.stack([cz, -sz * cx, sz * sx], axis=-1),
            jnp.stack([sz, cz * cx, -cz * sx], axis=-1),
            jnp.stack([zeros, sx, cx], axis=-1),
        ],
        axis=1,
    )
    points = icosa_points()
    rotated = matrix[:, :, 0, None] * points[None, 0, :]
    rotated = rotated + matrix[:, :, 1, None] * points[None, 1, :]
    rotated = rotated + matrix[:, :, 2, None] * points[None, 2, :]
    return rotated.reshape(count, -1)


def nonlocal_energy(elec_pos, atom_pos, quad_ratio, rotation, channels, ecp_coef, ecp_expo):
    walkers, electrons = rotation.shape
    count = NROT
    table = rotation_table(count)
    onehot = (rotation[:, :, None] == jnp.arange(count, dtype=jnp.int32)[None, None, :]).astype(
        jnp.float32
    )
    rotated = jnp.einsum("wek,kf->wef", onehot, table, precision=lax.Precision.HIGHEST)
    rotated = rotated.reshape(walkers, electrons, 3, -1)
    diff = elec_pos[:, :, None, :] - atom_pos[None, :, :, None]
    dist2 = jnp.sum(diff * diff, axis=1)
    unit = diff / jnp.sqrt(dist2 + 0.01)[:, None, :, :]
    cosang = unit[:, 0, :, :, None] * rotated[:, None, :, 0, :]
    cosang = cosang + unit[:, 1, :, :, None] * rotated[:, None, :, 1, :]
    cosang = cosang + unit[:, 2, :, :, None] * rotated[:, None, :, 2, :]
    quad = quad_ratio.shape[-1]
    lmax = ecp_coef.shape[1]
    lower = jnp.ones_like(cosang)
    upper = cosang
    total = jnp.zeros((walkers,), jnp.float32)
    for level in range(lmax):
        if level == 0:
            poly = lower
        elif level == 1:
            poly = upper
        else:
            fresh = ((2 * level - 1) * cosang * upper - (level - 1) * lower) / level
            lower, upper = (upper, fresh)
            poly = fresh
        angular = jnp.sum(poly * quad_ratio, axis=-1) / quad
        active = (channels > level).astype(jnp.float32)
        radial = ecp_coef[None, :, level, None] * jnp.exp(-ecp_expo[None, :, level, None] * dist2)
        term = (2 * level + 1) * active[None, :, None] * radial * angular
        total = total + jnp.sum(term, axis=(1, 2))
    return total


def sum_pieces(first, second):
    first_sum, second_sum = lax.psum((first, second), ("walk", "col"))
    return (first_sum, second_sum)


def body(
    jacobian,
    prev_update,
    base_energy,
    elec_pos,
    atom_pos,
    quad_ratio,
    rotation,
    channels,
    ecp_coef,
    ecp_expo,
):
    energy_mine = base_energy + nonlocal_energy(
        elec_pos, atom_pos, quad_ratio, rotation, channels, ecp_coef, ecp_expo
    )
    columns = lax.all_to_all(jacobian, "walk", split_axis=1, concat_axis=0, tiled=True)
    walkers = columns.shape[0]
    params_total = columns.shape[1] * lax.axis_size("walk") * lax.axis_size("col")
    scale = 1.0 / params_total
    centred = columns - jnp.mean(columns, axis=0, keepdims=True)
    prev_mine = prev_update[0]
    gram_part = (
        jnp.dot(
            centred, centred.T, precision=lax.Precision.HIGHEST, preferred_element_type=jnp.float32
        )
        * scale
    )
    along_part = (
        jnp.dot(
            centred, prev_mine, precision=lax.Precision.HIGHEST, preferred_element_type=jnp.float32
        )
        * scale
    )
    extra = along_part[:, None]
    gram, extra_sum = sum_pieces(gram_part, extra)
    along = extra_sum[:, 0]
    energies = lax.all_gather(energy_mine, "walk", axis=0, tiled=True)
    eps = -(energies - jnp.mean(energies)) / math.sqrt(walkers)
    system = gram + damping * jnp.eye(walkers, dtype=jnp.float32)
    factor = jnp.linalg.cholesky(system)
    solved = jax.scipy.linalg.cho_solve((factor, True), eps - momentum * along)
    update_mine = (
        jnp.dot(
            solved, centred, precision=lax.Precision.HIGHEST, preferred_element_type=jnp.float32
        )
        + momentum * prev_mine
    )
    return (energy_mine, update_mine[None, :])


def solution(mesh):
    in_specs = (
        P("walk", "col"),
        P("col", "walk"),
        P("walk"),
        P("walk", None, None),
        P(),
        P("walk", None, None, None),
        P("walk", None),
        P(),
        P(),
        P(),
    )
    out_specs = (P("walk"), P("col", "walk"))
    return jax.shard_map(body, mesh=mesh, in_specs=in_specs, out_specs=out_specs, check_vma=False)
```

profile of v0, /device:TPU:1, one launch (start us, length us, event | category | flops | bytes accessed | tf_op | source)
XLA Modules:
  0.0 826.4 jit_solution(6028116304954348564)
XLA Ops:
  7.3 19.4 %all-to-all-start = ((f32[6,64,1024]{2,0,1:T(8,128)}), f32[6,64,1024]{2,0,1:T(8,128)S(1)}, u32[]{:S(2)}, u32[]{:S(2)}) async-start(f32[6,64,1024]{2,0,1:T(8,128)} %bitcast.162), calls=%async_computation | async-start | bytes 4194304 | tf_op jit(solution)/shard_map/all_to_all | solution.py:103
  27.3 0.1 mul.376
  27.6 0.1 mul.384
  27.8 0.1 mul.392
  27.9 0.1 mul.379
  28.0 0.1 mul.387
  28.1 0.1 mul.395
  28.3 0.1 copy.26
  28.4 1.3 dynamic-slice.3
  30.4 0.1 fusion.13
  30.6 0.2 fusion.28
  30.8 0.1 subtract_divide_fusion
  30.9 0.6 multiply_reduce_fusion
  31.5 0.3 multiply_reduce_fusion.2
  31.8 0.5 fusion.57
  32.3 187.9 %all-reduce.1 = f32[384]{0:T(512)S(1)} all-reduce(f32[384]{0:T(512)S(1)} %get-tuple-element.32), channel_id=1, replica_groups=mesh['walk'=64,'col'=8] {'walk'}, use_global_device_ids=true, to_apply=%add.1 | all-reduce | flops 384 | bytes 3072
  220.3 0.6 reduce_sum.89
  221.5 0.2 reduce_sum.88
  221.7 1.6 subtract_bitcast_fusion
  223.3 1.6 sub.49
  225.0 3.4 convolution_multiply_fusion
  228.4 1.4 convolution_reduce_fusion
  229.9 133.3 %psum.15 = f32[384,1]{0,1:T(1,128)S(1)} all-reduce(f32[384,1]{0,1:T(1,128)S(1)} %broadcast_in_dim.6), channel_id=1, replica_groups=mesh['walk'=64,'col'=8] {'walk','col'}, use_global_device_ids=true, to_apply=%region_16.17 | all-reduce | flops 384 | bytes 3072 | tf_op jit(solution)/shard_map/psum | solution.py:84
  363.3 355.0 %all-reduce.4.cloned.1.call-done = f32[384,384]{0,1:T(8,128)} async-done(((f32[384,384]{0,1:T(8,128)}), f32[384,384]{0,1:T(8,128)}) %all-reduce.4.cloned.1.call-update) | async-done | bytes 589840 | tf_op jit(solution)/shard_map/psum | solution.py:84
  718.2 1.2 select_add_fusion
  719.4 0.2 copy.29
  719.8 11.7 %cholesky.76 = f32[128,128]{1,0:T(8,128)S(1)} custom-call(f32[128,128]{1,0:T(8,128)S(1)} %cholesky.189), custom_call_target="Cholesky" | custom-call | tf_op jit(solution)/shard_map/jit(cholesky)/cholesky | solution.py:127
  731.5 9.8 %custom-call.26 = f32[1,128,128]{1,2,0:T(8,128)S(1)} custom-call(f32[1,128,128]{2,1,0:T(8,128)S(1)} %get-tuple-element.45), custom_call_target="InvertDiagBlocksLowerTriangular" | custom-call | tf_op jit(solution)/shard_map/jit(cholesky)/cholesky | solution.py:127
  741.3 0.3 fusion.17
  741.6 0.3 convolution_subtract_fusion
  741.9 0.1 copy.31
  742.0 0.1 copy.30
  742.1 11.7 %cholesky.160 = f32[128,128]{1,0:T(8,128)S(1)} custom-call(f32[128,128]{1,0:T(8,128)S(1)} %cholesky.193), custom_call_target="Cholesky" | custom-call | tf_op jit(solution)/shard_map/jit(cholesky)/cholesky | solution.py:127
  753.8 0.1 copy.32
  754.0 10.0 %custom-call.27 = f32[1,128,128]{1,2,0:T(8,128)S(1)} custom-call(f32[1,128,128]{2,1,0:T(8,128)S(1)} %get-tuple-element.43), custom_call_target="InvertDiagBlocksLowerTriangular" | custom-call | tf_op jit(solution)/shard_map/jit(cholesky)/cholesky | solution.py:127
  764.0 0.3 convolution_dynamic-update-slice_fusion
  764.3 0.4 convolution_subtract_fusion.1
  764.7 11.7 %cholesky.179 = f32[128,128]{1,0:T(8,128)S(1)} custom-call(f32[128,128]{1,0:T(8,128)S(1)} %convolution_subtract_fusion.1), custom_call_target="Cholesky" | custom-call | tf_op jit(solution)/shard_map/jit(cholesky)/cholesky | solution.py:127
  776.5 0.1 copy.34
  776.6 0.7 compare_reduce_fusion
  777.3 0.6 compare_reduce_fusion.1
  779.9 6.7 while.1
  780.0 0.6 fusion.71
  780.6 1.4 dynamic-slice.8
  782.0 0.1 copy.44
  782.2 0.6 fusion.71
  782.8 1.4 dynamic-slice.8
  784.2 0.1 copy.44
  784.4 0.6 fusion.71
  785.0 1.4 dynamic-slice.8
  786.5 0.1 copy.44
  786.6 29.5 %custom-call.28 = f32[3,128,128]{1,2,0:T(8,128)S(1)} custom-call(f32[3,128,128]{2,1,0:T(8,128)S(1)} %get-tuple-element.9), custom_call_target="InvertDiagBlocksLowerTriangular" | custom-call | tf_op jit(solution)/shard_map/jit(_cho_solve)/triangular_solve | solution.py:128
  816.1 0.2 fusion.25
  816.2 0.2 fusion.5
  816.4 0.2 fusion.26
  816.6 0.2 fusion.6
  816.8 0.2 convolution_bitcast_fusion.5
  816.9 0.2 convolution_bitcast_fusion.4
  817.1 0.2 fusion.2
  817.4 0.2 convolution_bitcast_fusion.2
  817.6 0.2 fusion.7
  817.8 0.2 convolution_bitcast_fusion
  818.0 0.9 fusion.33
  818.9 0.6 multiply_add_fusion.1
  (83 shorter events, 1.8 us)
Async XLA Ops:
  7.2 20.8 %copy-start.11 = (f32[12]{0:T(128)S(1)}, f32[12]{0:T(128)}, u32[]{:S(2)}) copy-start(f32[12]{0:T(128)} %constant.198) | copy-start | bytes 148
  7.2 20.9 %copy-start.10 = (f32[12]{0:T(128)S(1)}, f32[12]{0:T(128)}, u32[]{:S(2)}) copy-start(f32[12]{0:T(128)} %constant.200) | copy-start | bytes 148
  7.2 20.9 %copy-start.9 = (f32[12]{0:T(128)S(1)}, f32[12]{0:T(128)}, u32[]{:S(2)}) copy-start(f32[12]{0:T(128)} %constant.202) | copy-start | bytes 148
  7.2 21.2 %copy-start.3 = (f32[6,3,66]{2,1,0:T(4,128)S(1)}, f32[6,3,66]{2,1,0:T(4,128)}, u32[]{:S(2)}) copy-start(f32[6,3,66]{2,1,0:T(4,128)} %param.14) | copy-start | bytes 14260
  7.2 23.1 %copy-start.4 = (f32[3,21]{1,0:T(4,128)S(1)}, f32[3,21]{1,0:T(4,128)}, u32[]{:S(2)}) copy-start(f32[3,21]{1,0:T(4,128)} %param.15) | copy-start | bytes 760
  7.2 23.2 %copy-start.12 = (s32[21]{0:T(128)S(1)}, s32[21]{0:T(128)}, u32[]{:S(2)}) copy-start(s32[21]{0:T(128)} %param.18) | copy-start | bytes 256
  7.2 23.3 %copy-start.6 = (f32[21,3]{0,1:T(4,128)S(1)}, f32[21,3]{0,1:T(4,128)}, u32[]{:S(2)}) copy-start(f32[21,3]{0,1:T(4,128)} %param.20) | copy-start | bytes 760
  7.2 23.3 %copy-start.7 = (f32[21,3]{0,1:T(4,128)S(1)}, f32[21,3]{0,1:T(4,128)}, u32[]{:S(2)}) copy-start(f32[21,3]{0,1:T(4,128)} %param.19) | copy-start | bytes 760
  7.3 23.3 %copy-start.5 = (s32[6,66]{1,0:T(8,128)S(1)}, s32[6,66]{1,0:T(8,128)}, u32[]{:S(2)}) copy-start(s32[6,66]{1,0:T(8,128)} %param.17) | copy-start | bytes 4756
  7.3 214.3 %all-to-all-start = ((f32[6,64,1024]{2,0,1:T(8,128)}), f32[6,64,1024]{2,0,1:T(8,128)S(1)}, u32[]{:S(2)}, u32[]{:S(2)}) async-start(f32[6,64,1024]{2,0,1:T(8,128)} %bitcast.162), calls=%async_computation | async-start | bytes 4194304 | tf_op jit(solution)/shard_map/all_to_all | solution.py:103
  26.7 4.2 copy-start.1
  26.7 691.5 %all-reduce.4.cloned.1.call-start = ((), (), s32[]{:S(2)}) async-start(), calls=%async_computation.1 | async-start | bytes 1179648 | tf_op jit(solution)/shard_map/psum | solution.py:84
  30.5 1.2 copy-start.8
  225.0 3.5 copy-start.2
  718.2 1.4 copy-start
Sparse Core Ops, SparseCore 0:
  228.5 489.6 all-reduce.3
where the time goes:
time: 827 us; the launch traced here: 826 us
  waiting for transfers between devices  355 us (43%)
  blocking collectives  321 us (39%)
  other arithmetic  92.2 us (11%)
  starting transfers between devices  19.5 us (2%)
  between operations  17.8 us (2%)
  local copies, waits for them, and re-layouts  11.5 us (1%)
  matrix products  9.1 us (1%)
    psum x1, waiting for transfers between devices, sum_pieces(): first_sum, second_sum = lax.psum((first, second), ('walk', 'col'))  355 us
    unnamed x1, blocking collectives  188 us
    psum x1, blocking collectives, sum_pieces(): first_sum, second_sum = lax.psum((first, second), ('walk', 'col'))  133 us
    another operation x10, other arithmetic, body(): factor = jnp.linalg.cholesky(system)  56.4 us
    another operation x3, other arithmetic, body(): solved = jax.scipy.linalg.cho_solve((factor, True), eps - momentum * along)  29.5 us
    all_to_all x1, starting transfers between devices, body(): lax.all_to_all(jacobian, 'walk', split_axis=1, concat_axis=0, tiled=True)  19.4 us
  transfers between devices with their start and end apart: 2, of which 1 were waited for; matrix products, arithmetic and copies ran while one was open for 1% of the time, Pallas kernels for 0%

commit v1 on v0

--- a/solution.py
+++ b/solution.py
@@ -81,7 +81,7 @@
 
 
 def sum_pieces(first, second):
-    first_sum, second_sum = lax.psum((first, second), ("walk", "col"))
+    first_sum, second_sum = lax.psum(lax.psum((first, second), "col"), "walk")
     return (first_sum, second_sum)
 
 

time: 827 us -> 581 us (0.70); the launches traced: 826 us -> 572 us
  blocking collectives: 321 us -> 130 us
  waiting for transfers between devices: 355 us -> 289 us
    unnamed x1 -> x0, blocking collectives: 188 us -> none
    psum x1 -> x2, waiting for transfers between devices: 355 us -> 199 us  [sum_pieces(): first_sum, second_sum = lax.psum(lax.psum((first, second), 'col'), 'walk')]
    all_to_all x1, waiting for transfers between devices: 0.01 us -> 89.8 us  [body(): lax.all_to_all(jacobian, 'walk', split_axis=1, concat_axis=0, tiled=True)]
    psum x1 -> x2, blocking collectives: 133 us -> 130 us  [sum_pieces(): first_sum, second_sum = lax.psum(lax.psum((first, second), 'col'), 'walk')]
  transfers between devices with their start and end apart: 2 -> 3, of which waited for: 1 -> 3; matrix products, arithmetic and copies ran while one was open for 1% -> 1% of each run, Pallas kernels for 0% -> 0%
where the time goes in v1:
time: 581 us; the launch traced here: 572 us
  waiting for transfers between devices  289 us (50%)
  blocking collectives  130 us (22%)
  other arithmetic  93 us (16%)
  starting transfers between devices  19.5 us (3%)
  between operations  17.8 us (3%)
  local copies, waits for them, and re-layouts  13.3 us (2%)
  matrix products  9.1 us (2%)
    psum x2, waiting for transfers between devices, sum_pieces(): first_sum, second_sum = lax.psum(lax.psum((first, second), 'col'), 'walk')  199 us
    psum x2, blocking collectives, sum_pieces(): first_sum, second_sum = lax.psum(lax.psum((first, second), 'col'), 'walk')  130 us
    all_to_all x1, waiting for transfers between devices, body(): lax.all_to_all(jacobian, 'walk', split_axis=1, concat_axis=0, tiled=True)  89.8 us
    another operation x10, other arithmetic, body(): factor = jnp.linalg.cholesky(system)  56.4 us
    another operation x3, other arithmetic, body(): solved = jax.scipy.linalg.cho_solve((factor, True), eps - momentum * along)  30.4 us
    all_to_all x1, starting transfers between devices, body(): lax.all_to_all(jacobian, 'walk', split_axis=1, concat_axis=0, tiled=True)  19.4 us
  transfers between devices with their start and end apart: 3, of which 3 were waited for; matrix products, arithmetic and copies ran while one was open for 1% of the time, Pallas kernels for 0%

profile of v1, /device:TPU:1, one launch (start us, length us, event | category | flops | bytes accessed | tf_op | source)
XLA Modules:
  0.0 571.8 jit_solution(15054803942541235435)
XLA Ops:
  7.3 19.4 %all-to-all-start = ((f32[6,64,1024]{2,0,1:T(8,128)}), f32[6,64,1024]{2,0,1:T(8,128)S(1)}, u32[]{:S(2)}, u32[]{:S(2)}) async-start(f32[6,64,1024]{2,0,1:T(8,128)} %bitcast.162), calls=%async_computation | async-start | bytes 4194304 | tf_op jit(solution)/shard_map/all_to_all | solution.py:103
  27.6 0.1 mul.384
  27.8 0.1 mul.392
  28.3 0.1 copy.26
  28.4 1.3 dynamic-slice.3
  30.4 0.1 fusion.13
  30.6 0.2 fusion.28
  30.8 0.1 subtract_divide_fusion
  30.9 0.6 multiply_reduce_fusion
  31.5 0.3 multiply_reduce_fusion.2
  31.7 89.8 %all-to-all-done = f32[6,64,1024]{2,0,1:T(8,128)S(1)} async-done(((f32[6,64,1024]{2,0,1:T(8,128)}), f32[6,64,1024]{2,0,1:T(8,128)S(1)}, u32[]{:S(2)}, u32[]{:S(2)}) %all-to-all-start) | async-done | bytes 1572896 | tf_op jit(solution)/shard_map/all_to_all | solution.py:103
  121.5 0.2 reduce_sum.88
  121.7 1.6 subtract_bitcast_fusion
  123.3 1.6 sub.49
  125.0 3.4 convolution_multiply_fusion
  128.5 0.5 fusion.57
  129.1 71.8 %all-reduce.6.cloned.1.call-done = f32[384,384]{0,1:T(8,128)} async-done(((f32[384,384]{0,1:T(8,128)}), f32[384,384]{0,1:T(8,128)}) %all-reduce.6.cloned.1.call-update) | async-done | bytes 589840 | tf_op jit(solution)/shard_map/psum | solution.py:84
  200.9 1.4 convolution_reduce_fusion
  202.3 13.9 %psum.30 = f32[384,1]{0,1:T(1,128)S(1)} all-reduce(f32[384,1]{0,1:T(1,128)S(1)} %broadcast_in_dim.6), channel_id=1, replica_groups=mesh['walk'=64,'col'=8] {'col'}, use_global_device_ids=true, to_apply=%region_17.18 | all-reduce | flops 384 | bytes 3072 | tf_op jit(solution)/shard_map/psum | solution.py:84
  216.2 116.5 %all-reduce.2 = (f32[384,1]{0,1:T(1,128)S(1)}, f32[384]{0:T(512)S(1)}) all-reduce(f32[384,1]{0,1:T(1,128)S(1)} %psum.30, f32[384]{0:T(512)S(1)} %get-tuple-element.34), channel_id=1, replica_groups=mesh['walk'=64,'col'=8] {'walk'}, use_global_device_ids=true, to_apply=%region_18.19 | all-reduce | flops 768 | bytes 6144 | tf_op jit(solution)/shard_map/psum | solution.py:84
  332.7 0.6 reduce_sum.89
  334.0 127.0 %all-reduce.8.cloned.1.call-done = f32[384,384]{0,1:T(8,128)} async-done(((f32[384,384]{0,1:T(8,128)}), f32[384,384]{0,1:T(8,128)}) %all-reduce.8.cloned.1.call-update) | async-done | bytes 589840 | tf_op jit(solution)/shard_map/psum | solution.py:84
  461.0 1.2 select_add_fusion
  462.2 0.2 copy.29
  462.6 11.7 %cholesky.76 = f32[128,128]{1,0:T(8,128)S(1)} custom-call(f32[128,128]{1,0:T(8,128)S(1)} %cholesky.189), custom_call_target="Cholesky" | custom-call | tf_op jit(solution)/shard_map/jit(cholesky)/cholesky | solution.py:127
  474.3 9.8 %custom-call.26 = f32[1,128,128]{1,2,0:T(8,128)S(1)} custom-call(f32[1,128,128]{2,1,0:T(8,128)S(1)} %get-tuple-element.47), custom_call_target="InvertDiagBlocksLowerTriangular" | custom-call | tf_op jit(solution)/shard_map/jit(cholesky)/cholesky | solution.py:127
  484.1 0.3 fusion.17
  484.4 0.3 convolution_subtract_fusion
  484.7 0.1 copy.31
  484.9 11.7 %cholesky.160 = f32[128,128]{1,0:T(8,128)S(1)} custom-call(f32[128,128]{1,0:T(8,128)S(1)} %cholesky.193), custom_call_target="Cholesky" | custom-call | tf_op jit(solution)/shard_map/jit(cholesky)/cholesky | solution.py:127
  496.6 0.1 copy.32
  496.8 10.0 %custom-call.27 = f32[1,128,128]{1,2,0:T(8,128)S(1)} custom-call(f32[1,128,128]{2,1,0:T(8,128)S(1)} %get-tuple-element.45), custom_call_target="InvertDiagBlocksLowerTriangular" | custom-call | tf_op jit(solution)/shard_map/jit(cholesky)/cholesky | solution.py:127
  506.8 0.3 convolution_dynamic-update-slice_fusion
  507.1 0.4 convolution_subtract_fusion.1
  507.5 11.7 %cholesky.179 = f32[128,128]{1,0:T(8,128)S(1)} custom-call(f32[128,128]{1,0:T(8,128)S(1)} %convolution_subtract_fusion.1), custom_call_target="Cholesky" | custom-call | tf_op jit(solution)/shard_map/jit(cholesky)/cholesky | solution.py:127
  519.3 0.1 copy.34
  519.4 0.7 compare_reduce_fusion
  520.1 0.6 compare_reduce_fusion.1
  522.7 8.5 %while.1 = (s32[]{:T(128)}, f32[384,384]{0,1:T(8,128)S(1)}, s32[3,2]{0,1:T(2,128)S(1)}, f32[3,128,128]{2,1,0:T(8,128)}, s32[]{:T(128)}) while((s32[]{:T(128)}, f32[384,384]{0,1:T(8,128)S(1)}, s32[3,2]{0,1:T(2,128)S(1)}, f32[3,128,128]{2,1,0:T(8,128)}, s32[]{:T(128)}) %tuple.50), condition=%wide.while_cond, body=%wide.while_body.sunk | while | flops 2 | bytes 393829 | solution.py:128
  522.8 0.6 fusion.71
  523.4 1.4 dynamic-slice.8
  524.8 0.1 copy.44
  524.9 0.6 bitcast_dynamic-update-slice_fusion.2
  525.6 0.6 fusion.71
  526.2 1.4 dynamic-slice.8
  527.6 0.1 copy.44
  527.7 0.6 bitcast_dynamic-update-slice_fusion.2
  528.4 0.6 fusion.71
  529.0 1.4 dynamic-slice.8
  530.4 0.1 copy.44
  530.5 0.6 bitcast_dynamic-update-slice_fusion.2
  531.2 30.3 %custom-call.28 = f32[3,128,128]{1,2,0:T(8,128)S(1)} custom-call(f32[3,128,128]{2,1,0:T(8,128)} %get-tuple-element.9), custom_call_target="InvertDiagBlocksLowerTriangular" | custom-call | tf_op jit(solution)/shard_map/jit(_cho_solve)/triangular_solve | solution.py:128
  561.5 0.2 fusion.25
  561.6 0.2 fusion.5
  561.8 0.2 fusion.26
  562.0 0.2 fusion.6
  562.2 0.2 convolution_bitcast_fusion.5
  562.3 0.2 convolution_bitcast_fusion.4
  562.5 0.2 fusion.2
  562.7 0.2 convolution_bitcast_fusion.2
  563.0 0.2 fusion.7
  563.2 0.2 convolution_bitcast_fusion
  563.4 0.9 fusion.33
  564.3 0.6 multiply_add_fusion.1
  (86 shorter events, 2.2 us)
Async XLA Ops:
  7.2 20.8 %copy-start.11 = (f32[12]{0:T(128)S(1)}, f32[12]{0:T(128)}, u32[]{:S(2)}) copy-start(f32[12]{0:T(128)} %constant.198) | copy-start | bytes 148
  7.2 20.9 %copy-start.10 = (f32[12]{0:T(128)S(1)}, f32[12]{0:T(128)}, u32[]{:S(2)}) copy-start(f32[12]{0:T(128)} %constant.200) | copy-start | bytes 148
  7.2 20.9 %copy-start.9 = (f32[12]{0:T(128)S(1)}, f32[12]{0:T(128)}, u32[]{:S(2)}) copy-start(f32[12]{0:T(128)} %constant.202) | copy-start | bytes 148
  7.2 21.2 %copy-start.3 = (f32[6,3,66]{2,1,0:T(4,128)S(1)}, f32[6,3,66]{2,1,0:T(4,128)}, u32[]{:S(2)}) copy-start(f32[6,3,66]{2,1,0:T(4,128)} %param.14) | copy-start | bytes 14260
  7.2 23.1 %copy-start.4 = (f32[3,21]{1,0:T(4,128)S(1)}, f32[3,21]{1,0:T(4,128)}, u32[]{:S(2)}) copy-start(f32[3,21]{1,0:T(4,128)} %param.15) | copy-start | bytes 760
  7.2 23.2 %copy-start.12 = (s32[21]{0:T(128)S(1)}, s32[21]{0:T(128)}, u32[]{:S(2)}) copy-start(s32[21]{0:T(128)} %param.18) | copy-start | bytes 256
  7.2 23.3 %copy-start.6 = (f32[21,3]{0,1:T(4,128)S(1)}, f32[21,3]{0,1:T(4,128)}, u32[]{:S(2)}) copy-start(f32[21,3]{0,1:T(4,128)} %param.20) | copy-start | bytes 760
  7.2 23.3 %copy-start.7 = (f32[21,3]{0,1:T(4,128)S(1)}, f32[21,3]{0,1:T(4,128)}, u32[]{:S(2)}) copy-start(f32[21,3]{0,1:T(4,128)} %param.19) | copy-start | bytes 760
  7.3 23.3 %copy-start.5 = (s32[6,66]{1,0:T(8,128)S(1)}, s32[6,66]{1,0:T(8,128)}, u32[]{:S(2)}) copy-start(s32[6,66]{1,0:T(8,128)} %param.17) | copy-start | bytes 4756
  7.3 114.3 %all-to-all-start = ((f32[6,64,1024]{2,0,1:T(8,128)}), f32[6,64,1024]{2,0,1:T(8,128)S(1)}, u32[]{:S(2)}, u32[]{:S(2)}) async-start(f32[6,64,1024]{2,0,1:T(8,128)} %bitcast.162), calls=%async_computation | async-start | bytes 4194304 | tf_op jit(solution)/shard_map/all_to_all | solution.py:103
  26.7 4.2 copy-start.1
  26.7 174.1 %all-reduce.6.cloned.1.call-start = ((), (), s32[]{:S(2)}) async-start(), calls=%async_computation.1 | async-start | bytes 1179648 | tf_op jit(solution)/shard_map/psum | solution.py:84
  125.0 3.6 copy-start.8
  125.0 75.9 %copy-start.2 = (f32[1,1024]{1,0:T(1,128)S(1)}, f32[1,1024]{1,0:T(1,128)}, u32[]{:S(2)}) copy-start(f32[1,1024]{1,0:T(1,128)} %param.12) | copy-start | bytes 12292
  128.4 332.6 %all-reduce.8.cloned.1.call-start = ((), (), s32[]{:S(2)}) async-start(), calls=%async_computation.2 | async-start | bytes 1179648 | tf_op jit(solution)/shard_map/psum | solution.py:84
  461.0 1.4 copy-start
Sparse Core Ops, SparseCore 0:
  128.6 72.2 all-reduce.5
  204.2 256.7 all-reduce.7
